TPU v7x, 512 devices: a whole 4x4x16 slice. The times are simulated.
512 devices in a mesh: segment: 2 (over core), lat: 64 (over x, z_lo, y), tok: 4 (over z_hi).
Axes of the slice: x: 4, y: 4, z: 16 (z_hi: 4, z_lo: 4; z = z_hi * 4 + z_lo), core: 2. Of those that a mesh axis runs over, the one named last changes fastest.
Arguments:
- resid_mid: bfloat16 [512, 4608], P('lat', ('segment', 'tok'))
- mlp_out: bfloat16 [512, 4608], P('lat', ('segment', 'tok'))
- post_gain: float32 [4608], P(('segment', 'tok')), may hold values from 0.5 to 1.5
- enc_weight: bfloat16 [4608, 65536], P(('segment', 'tok'), 'lat'), may hold values from -0.09375 to 0.09375
- enc_bias: float32 [65536], P('lat'), may hold values from -3 to 3
- dec_weight: bfloat16 [65536, 4608], P('lat', ('segment', 'tok')), may hold values from -0.046875 to 0.046875
- dec_bias: float32 [4608], P(('segment', 'tok')), may hold values from -3 to 3
- panel_lists: int32 [4, 128], replicated, may hold values from 0 to 511, as said below
Outputs:
- sq_error: float32 [], replicated
- enc_grad: bfloat16 [4608, 65536], P(('segment', 'tok'), 'lat')
- dec_grad: bfloat16 [65536, 4608], P('lat', ('segment', 'tok'))
Inputs may be any that keep to these rules, and one draw needn't show every extreme that they name: `panel_lists`: each row lists 128 different panels.
All inputs are finite; a program needn't handle non-finite values.
Results may differ from a plain program's by a relative error of at most 0.014.
Values may be sent and summed in bfloat16 or wider, within the bound.
A program may use at most 64 MiB of HBM per device.

v0:
```python
import jax
import jax.numpy as jnp
from jax import lax
from jax.sharding import PartitionSpec as P

D = 4608
PANEL = 128
BLOCK = 128


def gelu_pair(preact):
    activation, pullback = jax.vjp(jax.nn.gelu, preact)
    return (activation, pullback(jnp.ones_like(preact))[0])


def on_device(
    resid_mid, mlp_out, post_gain, enc_weight, enc_bias, dec_weight, dec_bias, panel_lists
):
    model_rows = mlp_out.astype(jnp.float32)
    squares_part = jnp.sum(model_rows * model_rows, axis=1)
    squares_total = lax.psum(squares_part, ("segment", "tok"))
    scale_rows = lax.rsqrt(squares_total / D + 1e-06)
    normed = model_rows * scale_rows[:, None] * post_gain[None, :]
    own_rows = (resid_mid.astype(jnp.float32) + normed).astype(jnp.bfloat16)
    features = lax.all_gather(own_rows, "lat", axis=0, tiled=True)
    token_count = features.shape[0]
    centered = (features.astype(jnp.float32) - dec_bias[None, :]).astype(jnp.bfloat16)
    encode_part = jnp.dot(centered, enc_weight, preferred_element_type=jnp.float32)
    preact = (
        lax.psum(encode_part.astype(jnp.bfloat16), ("segment", "tok")).astype(jnp.float32)
        + enc_bias[None, :]
    )
    panel_count = enc_weight.shape[1] // PANEL
    block_count = token_count // BLOCK
    panel_ids = lax.axis_index("lat") * panel_count + jnp.arange(panel_count, dtype=jnp.int32)
    active_flags = jnp.any(panel_lists[:, :, None] == panel_ids[None, None, :], axis=1).astype(
        jnp.float32
    )
    tile_mask = jnp.broadcast_to(
        active_flags[:, None, :, None], (block_count, BLOCK, panel_count, PANEL)
    ).reshape(token_count, enc_weight.shape[1])
    activation, derivative = gelu_pair(preact)
    latents = (activation * tile_mask).astype(jnp.bfloat16)
    decode_part = jnp.dot(latents, dec_weight, preferred_element_type=jnp.float32)
    rebuilt = lax.psum(decode_part, "lat") + dec_bias[None, :]
    error_full = rebuilt - features.astype(jnp.float32)
    error_sum = lax.psum(jnp.sum(error_full * error_full), ("segment", "tok"))
    error_bf = error_full.astype(jnp.bfloat16)
    sq_error = error_sum / (token_count * D)
    dec_grad = jnp.einsum(
        "tl,td->ld", latents, error_bf, preferred_element_type=jnp.float32
    ).astype(jnp.bfloat16)
    latent_part = jnp.einsum("td,ld->tl", error_bf, dec_weight, preferred_element_type=jnp.float32)
    latent_grad = lax.psum(latent_part.astype(jnp.bfloat16), ("segment", "tok")).astype(jnp.float32)
    pre_grad = (latent_grad * derivative * tile_mask).astype(jnp.bfloat16)
    enc_grad = jnp.einsum(
        "td,tl->dl", centered, pre_grad, preferred_element_type=jnp.float32
    ).astype(jnp.bfloat16)
    return (sq_error, enc_grad, dec_grad)


def solution(mesh):
    placed = (
        P("lat", ("segment", "tok")),
        P("lat", ("segment", "tok")),
        P(("segment", "tok")),
        P(("segment", "tok"), "lat"),
        P("lat"),
        P("lat", ("segment", "tok")),
        P(("segment", "tok")),
        P(),
    )
    return jax.shard_map(
        on_device,
        mesh=mesh,
        in_specs=placed,
        out_specs=(P(), P(("segment", "tok"), "lat"), P("lat", ("segment", "tok"))),
        check_vma=False,
    )
```

profile of v0, /device:TPU:15, one launch (start us, length us, event | category | flops | bytes accessed | tf_op | source)
XLA Modules:
  0.0 1230.6 jit_solution(12697475132606442277)
XLA Ops:
  7.2 0.0 copy-start
  7.2 0.0 all-reduce.4.cloned.1.call-start
  7.2 0.9 fusion.17
  8.1 30.3 %psum.35 = f32[8]{0:T(128)S(1)} all-reduce(f32[8]{0:T(128)S(1)} %fusion.17), channel_id=1, replica_groups=mesh['segment'=2,'lat'=64,'tok'=4] {'segment','tok'}, use_global_device_ids=true, to_apply=%region_1.0 | all-reduce | flops 8 | bytes 64 | tf_op jit(solution)/shard_map/psum | solution.py:21
  38.5 0.8 fusion.20
  39.3 135.7 %all_gather.3 = bf16[512,576]{1,0:T(8,128)(2,1)S(1)} all-gather(bf16[8,576]{1,0:T(8,128)(2,1)S(1)} %fusion.20), channel_id=1, replica_groups=mesh['segment'=2,'lat'=64,'tok'=4] {'lat'}, dimensions={0}, use_global_device_ids=true | all-gather | bytes 599040 | tf_op jit(solution)/shard_map/all_gather | solution.py:25
  175.0 0.2 copy.16
  175.2 0.0 copy-start.1
  175.3 0.0 copy-start.7
  175.3 3.6 convolution_convert_fusion.3
  178.8 0.0 copy-done.1
  178.8 0.0 all-reduce.4.cloned.1.call-update
  178.9 0.0 all-reduce.6.cloned.1.call-start
  178.9 0.0 copy-done.7
  178.9 0.2 compare_reduce_fusion
  179.2 190.6 %all-reduce.4.cloned.1.call-done = bf16[512,1024]{1,0:T(8,128)(2,1)} async-done(((bf16[512,1024]{1,0:T(8,128)(2,1)}), bf16[512,1024]{1,0:T(8,128)(2,1)}) %all-reduce.4.cloned.1.call-update) | async-done | bytes 1048592 | tf_op jit(solution)/shard_map/psum | solution.py:30
  369.8 0.2 broadcast_in_dim.2
  370.0 1.0 copy-done.2
  371.0 1.0 fusion.9
  372.0 1.0 copy-done.3
  372.9 1.8 fusion.27
  374.8 0.0 all-reduce.6.cloned.1.call-update
  374.8 0.0 all-reduce.8.cloned.1.call-start
  374.8 630.7 %all-reduce.6.cloned.1.call-done = f32[512,576]{0,1:T(8,128)} async-done(((f32[512,576]{0,1:T(8,128)}), f32[512,576]{0,1:T(8,128)}) %all-reduce.6.cloned.1.call-update) | async-done | bytes 1179664 | tf_op jit(solution)/shard_map/psum | solution.py:45
  1005.6 2.5 fusion.14
  1008.1 0.8 copy-done.4
  1008.9 2.0 convolution_convert_fusion.2
  1010.9 0.0 all-reduce.8.cloned.1.call-update
  1010.9 66.1 %psum.38 = f32[]{:T(128)} all-reduce(f32[]{:T(128)} %get-tuple-element.4), channel_id=1, replica_groups=mesh['segment'=2,'lat'=64,'tok'=4] {'segment','tok'}, use_global_device_ids=true, to_apply=%region_6.0 | all-reduce | flops 1 | bytes 8 | tf_op jit(solution)/shard_map/psum | solution.py:47
  1077.6 3.2 convolution_convert_fusion
  1080.8 137.0 %all-reduce.8.cloned.1.call-done = bf16[512,1024]{1,0:T(8,128)(2,1)} async-done(((bf16[512,1024]{1,0:T(8,128)(2,1)}), bf16[512,1024]{1,0:T(8,128)(2,1)}) %all-reduce.8.cloned.1.call-update) | async-done | bytes 1048592 | tf_op jit(solution)/shard_map/psum | solution.py:54
  1217.8 5.1 convolution_convert_fusion.1
  (11 shorter events, 0.0 us)
Async XLA Ops:
  7.2 365.8 %copy-start = (bf16[1024,576]{0,1:T(8,128)(2,1)S(1)}, bf16[1024,576]{0,1:T(8,128)(2,1)}, u32[]{:S(2)}) copy-start(bf16[1024,576]{0,1:T(8,128)(2,1)} %param.13) | copy-start | bytes 3538948
  7.2 362.6 %all-reduce.4.cloned.1.call-start = ((), (), s32[]{:S(2)}) async-start(), calls=%async_computation | async-start | bytes 2097152 | tf_op jit(solution)/shard_map/psum | solution.py:30
  175.2 3.6 copy-start.1
  175.3 3.7 copy-start.7
  178.8 191.1 %copy-start.5 = (f32[1024]{0:T(1024)S(1)}, f32[1024]{0:T(1024)}, u32[]{:S(2)}) copy-start(f32[1024]{0:T(1024)} %param.12) | copy-start | bytes 12292
  178.9 826.7 %all-reduce.6.cloned.1.call-start = ((), (), s32[]{:S(2)}) async-start(), calls=%async_computation.1 | async-start | bytes 2359296 | tf_op jit(solution)/shard_map/psum | solution.py:45
  369.8 1.2 copy-start.2
  371.9 1.0 copy-start.3
  372.9 632.7 %copy-start.6 = (f32[576]{0:T(1024)S(1)}, f32[576]{0:T(1024)}, u32[]{:S(2)}) copy-start(f32[576]{0:T(1024)} %param.14) | copy-start | bytes 6916
  374.8 843.0 %all-reduce.8.cloned.1.call-start = ((), (), s32[]{:S(2)}) async-start(), calls=%async_computation.2 | async-start | bytes 2097152 | tf_op jit(solution)/shard_map/psum | solution.py:54
  1008.1 0.8 copy-start.4
Sparse Core Ops, SparseCore 0:
  179.0 190.7 all-reduce.3
  374.9 630.6 all-reduce.5
  1011.0 206.7 all-reduce.7
where the time goes:
time: 1230 us
  waiting for transfers between devices  958 us (78%)
  blocking collectives  232 us (19%)
  matrix products  15.7 us (1%)
  between operations  15.6 us (1%)
    psum x1, waiting for transfers between devices, on_device(): rebuilt = lax.psum(decode_part, 'lat') + dec_bias[None, :]  631 us
    psum x1, waiting for transfers between devices, on_device(): lax.psum(encode_part.astype(jnp.bfloat16), ('segment', 'tok'))  191 us
    psum x1, waiting for transfers between devices, on_device(): lax.psum(latent_part.astype(jnp.bfloat16), ('segment', 'tok'))  137 us
    all_gather x1, blocking collectives, on_device(): features = lax.all_gather(own_rows, 'lat', axis=0, tiled=True)  136 us
    psum x1, blocking collectives, on_device(): error_sum = lax.psum(jnp.sum(error_full * error_full), ('segment', 'tok'))  66.1 us
    psum x1, blocking collectives, on_device(): squares_total = lax.psum(squares_part, ('segment', 'tok'))  30.3 us
  transfers between devices with their start and end apart: 3, of which 3 were waited for; matrix products, arithmetic and copies ran while one was open for 0% of the time, Pallas kernels for 0%

commit v1 on v0

--- a/solution.py
+++ b/solution.py
@@ -6,6 +6,11 @@
 D = 4608
 PANEL = 128
 BLOCK = 128
+
+
+def all_by_exchange(block, axis, dim):
+    sent = jnp.stack([block] * lax.axis_size(axis))
+    return jnp.concatenate(lax.all_to_all(sent, axis, 0, 0), axis=dim)
 
 
 def gelu_pair(preact):
@@ -22,7 +27,7 @@
     scale_rows = lax.rsqrt(squares_total / D + 1e-06)
     normed = model_rows * scale_rows[:, None] * post_gain[None, :]
     own_rows = (resid_mid.astype(jnp.float32) + normed).astype(jnp.bfloat16)
-    features = lax.all_gather(own_rows, "lat", axis=0, tiled=True)
+    features = all_by_exchange(own_rows, "lat", 0)
     token_count = features.shape[0]
     centered = (features.astype(jnp.float32) - dec_bias[None, :]).astype(jnp.bfloat16)
     encode_part = jnp.dot(centered, enc_weight, preferred_element_type=jnp.float32)

time: 1230 us -> 1080 us (0.88)
  blocking collectives: 232 us -> 122 us
  waiting for transfers between devices: 958 us -> 911 us
    all_gather x1 -> x0, blocking collectives: 136 us -> none  [on_device(): features = lax.all_gather(own_rows, 'lat', axis=0, tiled=True)]
    psum x1, waiting for transfers between devices: 191 us -> 143 us  [on_device(): lax.psum(encode_part.astype(jnp.bfloat16), ('segment', 'tok'))]
    all_to_all x0 -> x1, blocking collectives: none -> 26.1 us  [all_by_exchange(): return jnp.concatenate(lax.all_to_all(sent, axis, 0, 0), axis=dim)]
where the time goes in v1:
time: 1080 us; the launch traced here: 1070 us
  waiting for transfers between devices  911 us (84%)
  blocking collectives  122 us (11%)
  matrix products  16 us (1%)
  between operations  15.6 us (1%)
    psum x1, waiting for transfers between devices, on_device(): rebuilt = lax.psum(decode_part, 'lat') + dec_bias[None, :]  630 us
    psum x1, waiting for transfers between devices, on_device(): lax.psum(encode_part.astype(jnp.bfloat16), ('segment', 'tok'))  143 us
    psum x1, waiting for transfers between devices, on_device(): lax.psum(latent_part.astype(jnp.bfloat16), ('segment', 'tok'))  138 us
    psum x1, blocking collectives, on_device(): error_sum = lax.psum(jnp.sum(error_full * error_full), ('segment', 'tok'))  66.1 us
    psum x1, blocking collectives, on_device(): squares_total = lax.psum(squares_part, ('segment', 'tok'))  30.3 us
    all_to_all x1, blocking collectives, all_by_exchange(): return jnp.concatenate(lax.all_to_all(sent, axis, 0, 0), axis=dim)  26.1 us
  transfers between devices with their start and end apart: 3, of which 3 were waited for; matrix products, arithmetic and copies ran while one was open for 0% of the time, Pallas kernels for 0%

profile of v1, /device:TPU:15, one launch (start us, length us, event | category | flops | bytes accessed | tf_op | source)
XLA Modules:
  0.0 1075.0 jit_solution(1193891837666823515)
XLA Ops:
  7.2 0.0 copy-start
  7.2 0.0 all-reduce.4.cloned.1.call-start
  7.2 0.9 fusion.15
  8.1 30.3 %psum.35 = f32[8]{0:T(128)S(1)} all-reduce(f32[8]{0:T(128)S(1)} %fusion.15), channel_id=1, replica_groups=mesh['segment'=2,'lat'=64,'tok'=4] {'segment','tok'}, use_global_device_ids=true, to_apply=%region_1.0 | all-reduce | flops 8 | bytes 64 | tf_op jit(solution)/shard_map/psum | solution.py:26
  38.5 0.8 fusion.18
  39.3 0.1 stack.2
  39.3 26.1 %all_to_all.5 = bf16[64,8,576]{2,1,0:T(8,128)(2,1)S(1)} all-to-all(bf16[64,8,576]{2,1,0:T(8,128)(2,1)S(1)} %stack.2), channel_id=1, replica_groups=mesh['segment'=2,'lat'=64,'tok'=4] {'lat'}, dimensions={0} | all-to-all | bytes 1179648 | tf_op jit(solution)/shard_map/all_to_all | solution.py:13
  65.4 0.1 bitcast_convert_fusion
  65.5 1.4 copy.14
  66.9 0.0 copy-done.4
  66.9 3.7 convolution_convert_fusion.3
  70.6 0.0 all-reduce.4.cloned.1.call-update
  70.6 0.0 all-reduce.6.cloned.1.call-start
  70.7 0.2 compare_reduce_fusion
  70.9 142.7 %all-reduce.4.cloned.1.call-done = bf16[512,1024]{1,0:T(8,128)(2,1)} async-done(((bf16[512,1024]{1,0:T(8,128)(2,1)}), bf16[512,1024]{1,0:T(8,128)(2,1)}) %all-reduce.4.cloned.1.call-update) | async-done | bytes 1048592 | tf_op jit(solution)/shard_map/psum | solution.py:35
  213.7 0.2 broadcast_in_dim.2
  213.9 0.0 copy-done.5
  213.9 1.0 copy-done.1
  214.9 1.0 fusion.9
  215.9 1.0 copy-done.2
  216.9 1.8 fusion.25
  218.7 0.0 all-reduce.6.cloned.1.call-update
  218.7 0.0 all-reduce.8.cloned.1.call-start
  218.8 630.0 %all-reduce.6.cloned.1.call-done = f32[512,576]{0,1:T(8,128)} async-done(((f32[512,576]{0,1:T(8,128)}), f32[512,576]{0,1:T(8,128)}) %all-reduce.6.cloned.1.call-update) | async-done | bytes 1179664 | tf_op jit(solution)/shard_map/psum | solution.py:50
  848.8 2.7 multiply_reduce_fusion
  851.4 0.8 copy-done.3
  852.2 2.0 convolution_convert_fusion.2
  854.2 0.0 all-reduce.8.cloned.1.call-update
  854.3 66.1 %psum.38 = f32[]{:T(128)} all-reduce(f32[]{:T(128)} %get-tuple-element.3), channel_id=1, replica_groups=mesh['segment'=2,'lat'=64,'tok'=4] {'segment','tok'}, use_global_device_ids=true, to_apply=%region_6.0 | all-reduce | flops 1 | bytes 8 | tf_op jit(solution)/shard_map/psum | solution.py:52
  921.0 3.2 convolution_convert_fusion
  924.2 137.8 %all-reduce.8.cloned.1.call-done = bf16[512,1024]{1,0:T(8,128)(2,1)} async-done(((bf16[512,1024]{1,0:T(8,128)(2,1)}), bf16[512,1024]{1,0:T(8,128)(2,1)}) %all-reduce.8.cloned.1.call-update) | async-done | bytes 1048592 | tf_op jit(solution)/shard_map/psum | solution.py:59
  1062.0 5.3 convolution_convert_fusion.1
  (11 shorter events, 0.0 us)
Async XLA Ops:
  7.2 209.7 %copy-start = (bf16[1024,576]{0,1:T(8,128)(2,1)S(1)}, bf16[1024,576]{0,1:T(8,128)(2,1)}, u32[]{:S(2)}) copy-start(bf16[1024,576]{0,1:T(8,128)(2,1)} %param.13) | copy-start | bytes 3538948
  7.2 206.5 %all-reduce.4.cloned.1.call-start = ((), (), s32[]{:S(2)}) async-start(), calls=%async_computation.1 | async-start | bytes 2097152 | tf_op jit(solution)/shard_map/psum | solution.py:35
  65.4 1.5 copy-start.4
  66.9 3.8 copy-start.6
  70.6 143.3 %copy-start.5 = (f32[1024]{0:T(1024)S(1)}, f32[1024]{0:T(1024)}, u32[]{:S(2)}) copy-start(f32[1024]{0:T(1024)} %param.12) | copy-start | bytes 12292
  70.6 778.1 %all-reduce.6.cloned.1.call-start = ((), (), s32[]{:S(2)}) async-start(), calls=%async_computation.2 | async-start | bytes 2359296 | tf_op jit(solution)/shard_map/psum | solution.py:50
  213.7 1.2 copy-start.1
  215.9 1.0 copy-start.2
  218.7 843.3 %all-reduce.8.cloned.1.call-start = ((), (), s32[]{:S(2)}) async-start(), calls=%async_computation.3 | async-start | bytes 2097152 | tf_op jit(solution)/shard_map/psum | solution.py:59
  851.4 0.8 copy-start.3
Sparse Core Ops, SparseCore 0:
  70.8 142.8 all-reduce.3
  218.8 629.8 all-reduce.5
  854.4 207.6 all-reduce.7

commit v2 on v0

--- a/solution.py
+++ b/solution.py
@@ -1,3 +1,4 @@
+import functools
 import jax
 import jax.numpy as jnp
 from jax import lax
@@ -6,6 +7,15 @@
 D = 4608
 PANEL = 128
 BLOCK = 128
+
+
+def move_the_orders(obj, mesh_dim):
+    carry_in = lax.all_gather(obj, mesh_dim)
+    current_block = jnp.sum(carry_in, axis=0)
+    return current_block
+
+
+plan_wires_all = functools.partial(move_the_orders, mesh_dim=("segment", "tok"))
 
 
 def gelu_pair(preact):
@@ -18,7 +28,7 @@
 ):
     model_rows = mlp_out.astype(jnp.float32)
     squares_part = jnp.sum(model_rows * model_rows, axis=1)
-    squares_total = lax.psum(squares_part, ("segment", "tok"))
+    squares_total = plan_wires_all(squares_part)
     scale_rows = lax.rsqrt(squares_total / D + 1e-06)
     normed = model_rows * scale_rows[:, None] * post_gain[None, :]
     own_rows = (resid_mid.astype(jnp.float32) + normed).astype(jnp.bfloat16)

time: 1230 us -> 1230 us (level)
    psum x1 -> x0, blocking collectives: 30.3 us -> none  [on_device(): squares_total = lax.psum(squares_part, ('segment', 'tok'))]
    unnamed x0 -> x1, blocking collectives: none -> 30.3 us
where the time goes in v2:
time: 1230 us
  waiting for transfers between devices  960 us (78%)
  blocking collectives  232 us (19%)
  between operations  16.3 us (1%)
  matrix products  15.7 us (1%)
    psum x1, waiting for transfers between devices, on_device(): rebuilt = lax.psum(decode_part, 'lat') + dec_bias[None, :]  630 us
    psum x1, waiting for transfers between devices, on_device(): lax.psum(encode_part.astype(jnp.bfloat16), ('segment', 'tok'))  193 us
    psum x1, waiting for transfers between devices, on_device(): lax.psum(latent_part.astype(jnp.bfloat16), ('segment', 'tok'))  137 us
    all_gather x1, blocking collectives, on_device(): features = lax.all_gather(own_rows, 'lat', axis=0, tiled=True)  136 us
    psum x1, blocking collectives, on_device(): error_sum = lax.psum(jnp.sum(error_full * error_full), ('segment', 'tok'))  66.1 us
    unnamed x1, blocking collectives  30.3 us
  transfers between devices with their start and end apart: 3, of which 3 were waited for; matrix products, arithmetic and copies ran while one was open for 0% of the time, Pallas kernels for 0%

profile of v2, /device:TPU:15, one launch (start us, length us, event | category | flops | bytes accessed | tf_op | source)
XLA Modules:
  0.0 1234.4 jit_solution(14720920746668320095)
XLA Ops:
  7.2 0.0 copy-start
  7.2 0.0 all-reduce.5.cloned.1.call-start
  7.2 0.9 fusion.17
  8.1 1.3 dynamic-slice
  10.1 0.2 dynamic-update-slice
  10.3 30.3 %all-reduce = f32[64]{0:T(128)S(1)} all-reduce(f32[64]{0:T(128)S(1)} %dynamic-update-slice), channel_id=2, replica_groups=mesh['segment'=2,'lat'=64,'tok'=4] {'segment','tok'}, use_global_device_ids=true, to_apply=%add | all-reduce | flops 64 | bytes 512
  40.6 0.1 reshape.26
  40.8 0.8 fusion.20
  41.6 135.7 %all_gather.11 = bf16[512,576]{1,0:T(8,128)(2,1)S(1)} all-gather(bf16[8,576]{1,0:T(8,128)(2,1)S(1)} %fusion.20), channel_id=1, replica_groups=mesh['segment'=2,'lat'=64,'tok'=4] {'lat'}, dimensions={0}, use_global_device_ids=true | all-gather | bytes 599040 | tf_op jit(solution)/shard_map/all_gather | solution.py:35
  177.3 0.2 copy.16
  177.5 0.0 copy-start.7
  177.5 3.6 convolution_convert_fusion.3
  181.1 0.0 all-reduce.5.cloned.1.call-update
  181.1 0.0 all-reduce.7.cloned.1.call-start
  181.2 0.2 compare_reduce_fusion
  181.4 192.5 %all-reduce.5.cloned.1.call-done = bf16[512,1024]{1,0:T(8,128)(2,1)} async-done(((bf16[512,1024]{1,0:T(8,128)(2,1)}), bf16[512,1024]{1,0:T(8,128)(2,1)}) %all-reduce.5.cloned.1.call-update) | async-done | bytes 1048592 | tf_op jit(solution)/shard_map/psum | solution.py:40
  374.0 0.2 broadcast_in_dim.2
  374.2 1.0 copy-done.2
  375.2 1.0 fusion.9
  376.2 1.0 copy-done.3
  377.1 1.8 fusion.27
  379.0 0.0 all-reduce.7.cloned.1.call-update
  379.0 0.0 all-reduce.9.cloned.1.call-start
  379.0 630.0 %all-reduce.7.cloned.1.call-done = f32[512,576]{0,1:T(8,128)} async-done(((f32[512,576]{0,1:T(8,128)}), f32[512,576]{0,1:T(8,128)}) %all-reduce.7.cloned.1.call-update) | async-done | bytes 1179664 | tf_op jit(solution)/shard_map/psum | solution.py:55
  1009.1 2.5 fusion.14
  1011.6 0.8 copy-done.4
  1012.4 2.0 convolution_convert_fusion.2
  1014.4 0.0 all-reduce.9.cloned.1.call-update
  1014.4 66.1 %psum.30 = f32[]{:T(128)} all-reduce(f32[]{:T(128)} %get-tuple-element.4), channel_id=1, replica_groups=mesh['segment'=2,'lat'=64,'tok'=4] {'segment','tok'}, use_global_device_ids=true, to_apply=%region_6.0 | all-reduce | flops 1 | bytes 8 | tf_op jit(solution)/shard_map/psum | solution.py:57
  1081.1 3.2 convolution_convert_fusion
  1084.3 137.3 %all-reduce.9.cloned.1.call-done = bf16[512,1024]{1,0:T(8,128)(2,1)} async-done(((bf16[512,1024]{1,0:T(8,128)(2,1)}), bf16[512,1024]{1,0:T(8,128)(2,1)}) %all-reduce.9.cloned.1.call-update) | async-done | bytes 1048592 | tf_op jit(solution)/shard_map/psum | solution.py:64
  1221.7 5.1 convolution_convert_fusion.1
  (16 shorter events, 0.1 us)
Async XLA Ops:
  7.2 370.0 %copy-start = (bf16[1024,576]{0,1:T(8,128)(2,1)S(1)}, bf16[1024,576]{0,1:T(8,128)(2,1)}, u32[]{:S(2)}) copy-start(bf16[1024,576]{0,1:T(8,128)(2,1)} %param.13) | copy-start | bytes 3538948
  7.2 366.8 %all-reduce.5.cloned.1.call-start = ((), (), s32[]{:S(2)}) async-start(), calls=%async_computation | async-start | bytes 2097152 | tf_op jit(solution)/shard_map/psum | solution.py:40
  177.5 3.6 copy-start.1
  177.5 3.7 copy-start.7
  181.1 193.1 %copy-start.5 = (f32[1024]{0:T(1024)S(1)}, f32[1024]{0:T(1024)}, u32[]{:S(2)}) copy-start(f32[1024]{0:T(1024)} %param.12) | copy-start | bytes 12292
  181.1 827.9 %all-reduce.7.cloned.1.call-start = ((), (), s32[]{:S(2)}) async-start(), calls=%async_computation.1 | async-start | bytes 2359296 | tf_op jit(solution)/shard_map/psum | solution.py:55
  374.0 1.2 copy-start.2
  376.1 1.0 copy-start.3
  377.1 631.9 %copy-start.6 = (f32[576]{0:T(1024)S(1)}, f32[576]{0:T(1024)}, u32[]{:S(2)}) copy-start(f32[576]{0:T(1024)} %param.14) | copy-start | bytes 6916
  379.0 842.7 %all-reduce.9.cloned.1.call-start = ((), (), s32[]{:S(2)}) async-start(), calls=%async_computation.2 | async-start | bytes 2097152 | tf_op jit(solution)/shard_map/psum | solution.py:64
  1011.6 0.8 copy-start.4
Sparse Core Ops, SparseCore 0:
  181.3 192.6 all-reduce.4
  379.1 629.8 all-reduce.6
  1014.5 207.1 all-reduce.8
